TPU v7x, 512 devices: a whole 4x4x16 slice. The times are simulated.
512 devices in a mesh: dp: 32 (over x, y, core), mp: 16 (over z).
Axes of the slice: x: 4, y: 4, z: 16, core: 2. Of those that a mesh axis runs over, the one named last changes fastest.
Arguments:
- hidden: bfloat16 [65536, 4096], P('dp', 'mp'), may hold values from -600 to 600
- segments: int32 [512, 128], P('dp'), may hold values from 0 to 5, never falling along the last dimension, each value on 1 to 40 neighbouring positions
- counts: int32 [32], replicated, may hold values from 1 to 16, 256 in all
- dest_order: int32 [32], replicated, may hold values from 0 to 31, each once
- norm_gain: bfloat16 [4096], replicated, may hold values from 0.5 to 1.5
- q_weight: bfloat16 [4096, 4096], P(None, 'mp'), may hold values from -1.921875 to 1.921875
- kv_weight: bfloat16 [4096, 2048], P(None, 'mp'), may hold values from -0.09375 to 0.09375
Outputs:
- attended: bfloat16 [32768, 4096], P('dp', 'mp')
Inputs may be any that keep to these rules, and one draw needn't show every extreme that they name: counts sum to 256 and reach 16 on some index of dp. `segments`: ids never fall within a block; a hypothesis spans at most 40 tokens.
All inputs are finite; a program needn't handle non-finite values.
Results may differ from a plain program's by a relative error of at most 0.0073.
Values may be sent and summed in bfloat16 or wider, within the bound.
A program may use at most 64 MiB of HBM per device.

v0:
```python
import jax
import jax.numpy as jnp
from jax import lax
from jax.sharding import PartitionSpec as P

KV = 8
HD = 128


epsilon = 1e-05
rope_base = 500000.0


def total_of_pieces(array, axis):
    blocks = lax.all_gather(array, axis)
    return blocks.sum(axis=0)


def swapped(value, axis, stride):
    mask = 2**stride
    pairs = [(source, source ^ mask) for source in range(lax.axis_size(axis))]
    return lax.ppermute(value, axis, pairs)


def rope_tables(positions, width):
    halves = width // 2
    frequency = rope_base ** (-(jnp.arange(halves, dtype=jnp.float32) * 2.0) / width)
    angles = positions.astype(jnp.float32)[..., None] * frequency
    return (jnp.cos(angles), jnp.sin(angles))


def rotate(tensor, cosine, sine_part):
    halves = tensor.shape[-1] // 2
    lower = tensor[..., :halves]
    upper = tensor[..., halves:]
    cosine = cosine[..., None, :]
    sine_part = sine_part[..., None, :]
    return jnp.concatenate(
        [lower * cosine - upper * sine_part, upper * cosine + lower * sine_part], axis=-1
    )


def segment_masks(block_segments):
    length = block_segments.shape[-1]
    column = jnp.arange(length, dtype=jnp.int32)
    same_segment = block_segments[:, :, None] == block_segments[:, None, :]
    before = column[None, :] < column[:, None]
    positions = jnp.sum((same_segment & before[None]).astype(jnp.int32), axis=2)
    visible = same_segment & (column[None, :] <= column[:, None])[None]
    return (positions, visible)


def join_pieces(mine, theirs, upper_half):
    halves = mine.shape[-1] // 2
    leading = jnp.where(upper_half, theirs, mine)
    trailing = jnp.where(upper_half, mine, theirs)
    return jnp.concatenate(
        [leading[:, :halves], trailing[:, :halves], leading[:, halves:], trailing[:, halves:]],
        axis=-1,
    )


def on_device(hidden, segments, counts, dest_order, norm_gain, q_weight, kv_weight):
    dp_count = lax.axis_size("dp")
    mp_count = lax.axis_size("mp")
    dp_index = lax.axis_index("dp")
    mp_index = lax.axis_index("mp")
    in_slots = segments.shape[0]
    block_len = segments.shape[1]
    kept_slots = in_slots // 2
    per_peer = (in_slots + dp_count - 1) // dp_count
    local_width = hidden.shape[1]
    kv_local = max(1, KV // mp_count)
    token_count = kept_slots * block_len
    device_ids = jnp.arange(dp_count, dtype=jnp.int32)
    starts = jnp.cumsum(counts) - counts
    finishes = starts + counts
    position_of = jnp.sum(
        device_ids[None, :] * (dest_order[None, :] == device_ids[:, None]).astype(jnp.int32), axis=1
    )
    offsets = (position_of - starts[dp_index]) % dp_count
    wanted = offsets[:, None] + jnp.arange(per_peer, dtype=jnp.int32)[None, :] * dp_count
    usable = wanted < counts[dp_index]
    slot_ids = jnp.arange(in_slots, dtype=jnp.int32)
    choose = ((wanted[:, :, None] == slot_ids[None, None, :]) & usable[:, :, None]).astype(
        jnp.bfloat16
    )
    choose = choose.reshape(dp_count * per_peer, in_slots)
    outgoing = jnp.dot(
        choose,
        hidden.reshape(in_slots, block_len * local_width),
        preferred_element_type=jnp.float32,
    ).astype(jnp.bfloat16)
    segment_out = jnp.dot(
        choose, segments.astype(jnp.bfloat16), preferred_element_type=jnp.float32
    ).astype(jnp.bfloat16)
    global_ids = jnp.arange(kept_slots, dtype=jnp.int32) * dp_count + position_of[dp_index]
    sources = jnp.sum((finishes[None, :] <= global_ids[:, None]).astype(jnp.int32), axis=1)
    arrive_rows = sources * per_peer + (global_ids - starts[sources]) // dp_count
    place = (
        arrive_rows[:, None] == jnp.arange(dp_count * per_peer, dtype=jnp.int32)[None, :]
    ).astype(jnp.bfloat16)
    arrived, segment_in = (
        lax.all_to_all(outgoing, "dp", split_axis=0, concat_axis=0, tiled=True),
        lax.all_to_all(segment_out, "dp", split_axis=0, concat_axis=0, tiled=True),
    )
    rows = jnp.dot(place, arrived, preferred_element_type=jnp.float32).astype(jnp.bfloat16)
    rows = rows.reshape(token_count, local_width)
    block_segments = jnp.dot(place, segment_in, preferred_element_type=jnp.float32)
    widened = rows.astype(jnp.float32)
    partial_sums = jnp.sum(widened * widened, axis=1)
    totals = total_of_pieces(partial_sums, "mp")
    row_scale = lax.rsqrt(totals / norm_gain.shape[0] + epsilon)[:, None]
    local_gain = lax.dynamic_slice_in_dim(norm_gain, mp_index * local_width, local_width)
    gained = (widened * local_gain.astype(jnp.float32)).astype(jnp.bfloat16)
    normed = lax.all_gather(gained, "mp", axis=1, tiled=True)
    queries = row_scale * jnp.dot(normed, q_weight, preferred_element_type=jnp.float32)
    kv_rows = (row_scale * jnp.dot(normed, kv_weight, preferred_element_type=jnp.float32)).astype(
        jnp.bfloat16
    )
    theirs = swapped(kv_rows, "mp", 0)
    upper_half = mp_index // (1 << 0) % 2 == 1
    kv_rows = join_pieces(kv_rows, theirs, upper_half)
    kv_split = kv_rows.reshape(token_count, kv_local, 2, HD)
    key_raw = kv_split[:, :, 0, :]
    value_rows = kv_split[:, :, 1, :]
    positions, visible = segment_masks(block_segments)
    cosine, sine_part = rope_tables(positions, HD)
    q_heads = queries.shape[1] // HD
    query_rows = rotate(
        queries.reshape(kept_slots, block_len, q_heads, HD), cosine, sine_part
    ).astype(jnp.bfloat16)
    key_rows = rotate(
        key_raw.astype(jnp.float32).reshape(kept_slots, block_len, kv_local, HD), cosine, sine_part
    ).astype(jnp.bfloat16)
    grouped = query_rows.reshape(kept_slots, block_len, kv_local, q_heads // kv_local, HD)
    scores = jnp.einsum(
        "nikgd,njkd->nkgij", grouped, key_rows, preferred_element_type=jnp.float32
    ) * HD ** (-0.5)
    scores = jnp.where(visible[:, None, None], scores, -jnp.inf)
    highest = jnp.max(scores, axis=-1, keepdims=True)
    weights = jnp.exp(scores - highest)
    shares = (weights / jnp.sum(weights, axis=-1, keepdims=True)).astype(jnp.bfloat16)
    values = value_rows.reshape(kept_slots, block_len, kv_local, HD)
    mixture = jnp.einsum("nkgij,njkd->nikgd", shares, values, preferred_element_type=jnp.float32)
    return mixture.reshape(token_count, q_heads * HD).astype(jnp.bfloat16)


def solution(mesh):
    in_specs = (P("dp", "mp"), P("dp", None), P(), P(), P(), P(None, "mp"), P(None, "mp"))
    out_specs = P("dp", "mp")
    return jax.shard_map(
        on_device, mesh=mesh, in_specs=in_specs, out_specs=out_specs, check_vma=False
    )
```

profile of v0, /device:TPU:24, one launch (start us, length us, event | category | flops | bytes accessed | tf_op | source)
XLA Modules:
  0.0 241.3 jit_solution(16235751715637646904)
XLA Ops:
  6.5 1.7 reshape.286
  9.0 1.2 dynamic_slice.14
  12.5 1.3 broadcast_compare_fusion
  13.8 2.0 fusion
  16.4 4.6 %reduce.3 = bf16[32,32768]{1,0:T(8,128)(2,1)} reduce(bf16[32,1,32768]{2,0,1:T(8,128)(2,1)} %fusion, bf16[]{:T(256)} %broadcast.283), dimensions={1}, to_apply=%copy.45.reduce_sub_computation | reduce | bytes 4194306 | tf_op jit(solution)/shard_map/all_to_all | solution.py:104
  21.0 4.5 %reshape.306 = bf16[32,2,16384]{2,1,0:T(2,128)(2,1)} reshape(bf16[32,32768]{1,0:T(8,128)(2,1)} %reduce.3) | data formatting | bytes 4194304
  25.5 10.0 %all-to-all-start = ((bf16[32,2,16384]{2,1,0:T(2,128)(2,1)}), bf16[32,2,16384]{2,1,0:T(2,128)(2,1)}, u32[]{:S(2)}, u32[]{:S(2)}) async-start(bf16[32,2,16384]{2,1,0:T(2,128)(2,1)} %reshape.306), calls=%async_computation | async-start | bytes 4194304 | tf_op jit(solution)/shard_map/all_to_all | solution.py:104
  39.0 23.3 %all-to-all-done = bf16[32,2,16384]{2,1,0:T(2,128)(2,1)} async-done(((bf16[32,2,16384]{2,1,0:T(2,128)(2,1)}), bf16[32,2,16384]{2,1,0:T(2,128)(2,1)}, u32[]{:S(2)}, u32[]{:S(2)}) %all-to-all-start) | async-done | bytes 2097184 | tf_op jit(solution)/shard_map/all_to_all | solution.py:104
  62.3 10.5 %reshape.307 = bf16[32,1,32768]{2,1,0:T(2,128)(2,1)} reshape(bf16[32,2,16384]{2,1,0:T(2,128)(2,1)} %all-to-all-done) | data formatting | bytes 4194304
  72.8 5.5 %fusion.1 = f32[8,32768]{1,0:T(8,128)} fusion(bf16[32,1,32768]{2,1,0:T(2,128)(2,1)} %reshape.307, s32[8]{0:T(128)S(1)} %fusion.43), kind=kOutput, calls=%fused_computation.4 | convolution fusion | flops 17301760 | bytes 3145760 | tf_op jit(solution)/shard_map/dot_general | solution.py:107
  78.2 1.4 reshape.291
  81.4 5.8 %all-to-all-start.1 = ((bf16[32,1,128]{2,1,0:T(2,128)(2,1)}), bf16[32,1,128]{2,1,0:T(2,128)(2,1)S(1)}, u32[]{:S(2)}, u32[]{:S(2)}) async-start(bf16[32,1,128]{2,1,0:T(2,128)(2,1)} %copy.47), calls=%async_computation.1 | async-start | bytes 32768 | tf_op jit(solution)/shard_map/all_to_all | solution.py:105
  87.3 5.6 %all-to-all-done.1 = bf16[32,1,128]{2,1,0:T(2,128)(2,1)S(1)} async-done(((bf16[32,1,128]{2,1,0:T(2,128)(2,1)}), bf16[32,1,128]{2,1,0:T(2,128)(2,1)S(1)}, u32[]{:S(2)}, u32[]{:S(2)}) %all-to-all-start.1) | async-done | bytes 8224 | tf_op jit(solution)/shard_map/all_to_all | solution.py:105
  93.5 3.1 %multiply_cosine_fusion = (f32[8,128,64]{2,1,0:T(8,128)}, f32[8,128,64]{2,1,0:T(8,128)}) fusion(f32[64]{0:T(128)S(1)} %multiply_power_fusion, f32[8,128]{1,0:T(8,128)S(1)} %convert_element_type.93), kind=kLoop, calls=%fused_computation.25 | loop fusion | flops 65536 | bytes 528640 | tf_op jit(solution)/shard_map/cos | solution.py:29
  96.6 33.4 %all-gather = f32[16384]{0:T(1024)S(1)} all-gather(f32[1024]{0:T(1024)S(1)} %get-tuple-element.11), channel_id=2, replica_groups=mesh['dp'=32,'mp'=16] {'mp'}, dimensions={0}, use_global_device_ids=true | all-gather | bytes 69632 | tf_op jit(solution)/shard_map/all_gather | solution.py:15
  130.1 78.8 %all-gather.3.cloned.1.call-done = bf16[1024,4096]{1,0:T(8,128)(2,1)} async-done(((bf16[1024,256]{1,0:T(8,128)(2,1)}), bf16[1024,4096]{1,0:T(8,128)(2,1)}) %all-gather.3.cloned.1.call-update) | async-done | bytes 8388624 | tf_op jit(solution)/shard_map/all_gather | solution.py:116
  208.8 6.7 %fusion.7 = bf16[1024,128]{0,1:T(8,128)(2,1)S(1)} fusion(bf16[1024,4096]{1,0:T(8,128)(2,1)} %all-gather.3.cloned.1.call-done, bf16[4096,128]{1,0:T(8,128)(2,1)} %param.13, f32[1024]{0:T(1024)S(1)} %add_rsqrt_fusion), kind=kOutput, calls=%fused_computation.14 | convolution fusion | flops 1074003968 | bytes 9703424 | tf_op jit(solution)/shard_map/dot_general | solution.py:118
  215.5 3.8 %collective-permute-start = (bf16[1024,128]{0,1:T(8,128)(2,1)S(1)}, bf16[1024,128]{0,1:T(8,128)(2,1)}, u32[]{:S(2)}, u32[]{:S(2)}) collective-permute-start(bf16[1024,128]{0,1:T(8,128)(2,1)S(1)} %fusion.7), channel_id=1, source_target_pairs={{0,1},{1,0},{2,3},{3,2},{4,5},{5,4},{6,7},{7,6},{8,9},{9,8},{10,11... | collective-permute-start | bytes 786440 | tf_op jit(solution)/shard_map/ppermute | solution.py:22
  219.3 3.3 %convolution_multiply_fusion.1 = f32[1024,256]{1,0:T(8,128)} fusion(bf16[1024,4096]{1,0:T(8,128)(2,1)S(1)} %copy-done.1, bf16[4096,256]{1,0:T(8,128)(2,1)S(1)} %copy-done, f32[1024]{0:T(1024)S(1)} %add_rsqrt_fusion), kind=kOutput, calls=%fused_computation.9 | convolution fusion | flops 2147745792 | bytes 11538432 | tf_op jit(solution)/shard_map/dot_general | solution.py:117
  222.6 1.7 reshape.289
  224.4 1.2 fusion.45
  225.6 1.3 subtract_convert_fusion
  228.4 2.4 fusion.25
  230.8 1.8 fusion.48
  (51 shorter events, 12.8 us)
Async XLA Ops:
  6.5 212.7 %copy-start = (bf16[4096,256]{1,0:T(8,128)(2,1)S(1)}, bf16[4096,256]{1,0:T(8,128)(2,1)}, u32[]{:S(2)}) copy-start(bf16[4096,256]{1,0:T(8,128)(2,1)} %param.12) | copy-start | bytes 6291460
  25.5 36.8 %all-to-all-start = ((bf16[32,2,16384]{2,1,0:T(2,128)(2,1)}), bf16[32,2,16384]{2,1,0:T(2,128)(2,1)}, u32[]{:S(2)}, u32[]{:S(2)}) async-start(bf16[32,2,16384]{2,1,0:T(2,128)(2,1)} %reshape.306), calls=%async_computation | async-start | bytes 4194304 | tf_op jit(solution)/shard_map/all_to_all | solution.py:104
  35.4 173.4 %all-gather.3.cloned.1.call-start = ((), (), s32[]{:S(2)}) async-start(), calls=%async_computation.2 | async-start | bytes 8912896 | tf_op jit(solution)/shard_map/all_gather | solution.py:116
  72.8 7.8 %copy-start.4 = (s32[16,128]{1,0:T(8,128)S(1)}, s32[16,128]{1,0:T(8,128)}, u32[]{:S(2)}) copy-start(s32[16,128]{1,0:T(8,128)} %param.8) | copy-start | bytes 24580
  81.4 11.5 %all-to-all-start.1 = ((bf16[32,1,128]{2,1,0:T(2,128)(2,1)}), bf16[32,1,128]{2,1,0:T(2,128)(2,1)S(1)}, u32[]{:S(2)}, u32[]{:S(2)}) async-start(bf16[32,1,128]{2,1,0:T(2,128)(2,1)} %copy.47), calls=%async_computation.1 | async-start | bytes 32768 | tf_op jit(solution)/shard_map/all_to_all | solution.py:105
  208.8 10.5 %copy-start.1 = (bf16[1024,4096]{1,0:T(8,128)(2,1)S(1)}, bf16[1024,4096]{1,0:T(8,128)(2,1)}, u32[]{:S(2)}) copy-start(bf16[1024,4096]{1,0:T(8,128)(2,1)} %all-gather.3.cloned.1.call-done) | copy-start | bytes 25165828
  215.5 11.4 %collective-permute-start = (bf16[1024,128]{0,1:T(8,128)(2,1)S(1)}, bf16[1024,128]{0,1:T(8,128)(2,1)}, u32[]{:S(2)}, u32[]{:S(2)}) collective-permute-start(bf16[1024,128]{0,1:T(8,128)(2,1)S(1)} %fusion.7), channel_id=1, source_target_pairs={{0,1},{1,0},{2,3},{3,2},{4,5},{5,4},{6,7},{7,6},{8,9},{9,8},{10,11... | collective-permute-start | bytes 786440 | tf_op jit(solution)/shard_map/ppermute | solution.py:22
  224.4 1.2 copy-start.2
  224.4 1.2 copy-start.3
Sparse Core Ops, SparseCore 0:
  80.7 128.1 all-gather.2
where the time goes:
time: 245 us; the launch traced here: 241 us
  waiting for transfers between devices  108 us (44%)
  blocking collectives  33.4 us (14%)
  local copies, waits for them, and re-layouts  27.7 us (11%)
  matrix products  20.1 us (8%)
  starting transfers between devices  19.6 us (8%)
  other arithmetic  19.2 us (8%)
  between operations  13.7 us (6%)
    all_gather x1, waiting for transfers between devices, on_device(): normed = lax.all_gather(gained, 'mp', axis=1, tiled=True)  78.8 us
    all_gather x1, blocking collectives, total_of_pieces(): blocks = lax.all_gather(array, axis)  33.4 us
    all_to_all x1, waiting for transfers between devices, on_device(): lax.all_to_all(outgoing, 'dp', split_axis=0, concat_axis=0, tiled=True)  23.3 us
    unnamed x14, local copies, waits for them, and re-layouts  16 us
    all_to_all x1, starting transfers between devices, on_device(): lax.all_to_all(outgoing, 'dp', split_axis=0, concat_axis=0, tiled=True)  9.96 us
    dot_general x1, matrix products, on_device(): jnp.dot(normed, kv_weight, preferred_element_type=jnp.float32)  6.66 us
    all_to_all x1, starting transfers between devices, on_device(): lax.all_to_all(segment_out, 'dp', split_axis=0, concat_axis=0, tiled=True)  5.85 us
    all_to_all x1, waiting for transfers between devices, on_device(): lax.all_to_all(segment_out, 'dp', split_axis=0, concat_axis=0, tiled=True)  5.56 us
  transfers between devices with their start and end apart: 4, of which 3 were waited for; matrix products, arithmetic and copies ran while one was open for 6% of the time, Pallas kernels for 0%

commit v1 on v0

v1 whole, which is shorter than its diff:
```python
import functools

import jax
import jax.numpy as jnp
import numpy as np
from jax import lax
from jax.experimental import pallas as pl
from jax.experimental.pallas import tpu as pltpu
from jax.sharding import PartitionSpec as P

HD = 128
HALF = HD // 2
GROUPS = 4
epsilon = 1e-05
rope_base = 500000.0
MASKED = -1e30
MESH = pl.DeviceIdType.MESH
f32 = jnp.float32
bf16 = jnp.bfloat16


def rope_table(length):
    frequency = rope_base ** (-(np.arange(HALF, dtype=np.float32) * 2.0) / HD)
    angles = np.arange(length, dtype=np.float32)[:, None] * frequency.astype(np.float32)
    cosine, sine = np.cos(angles), np.sin(angles)
    return np.concatenate([cosine, cosine, -sine, sine], axis=1).astype(np.float32)


def kernel(
    n_dp, n_mp, hidden, segments, counts, dest, gain, q_weight, kv_weight, table, out,
    hid, seg, wq, wkv, send, seg_send, seg_recv, recv0, recv1, recv2, recv3,
    ag, acc, squares, kv_mine, kv_theirs, q_rot, keys, values, tables, masks, gains, slots, sources,
    local_sem, send_sem, move_sem, seg_sem, ring_send, ring_recv, kv_send, kv_recv,
):
    recvs = (recv0, recv1, recv2, recv3)
    me_d = lax.axis_index("dp")
    me_z = lax.axis_index("mp")
    in_slots, block_len, width = hid.shape
    kept = in_slots // 2
    rows = block_len // GROUPS
    group_rows = kept * rows
    piece = group_rows // 2
    far = n_mp // 2
    near = far // 2
    right = lax.rem(me_z + 1, n_mp)
    left = lax.rem(me_z + n_mp - 1, n_mp)
    odd = lax.rem(me_z, 2)
    partner = me_z + 1 - 2 * odd

    local = [
        pltpu.make_async_copy(hidden, hid, local_sem.at[0]),
        pltpu.make_async_copy(segments, seg, local_sem.at[1]),
        pltpu.make_async_copy(q_weight, wq, local_sem.at[2]),
        pltpu.make_async_copy(kv_weight, wkv, local_sem.at[3]),
    ]
    for copy in local:
        copy.start()

    barrier = pltpu.get_barrier_semaphore()

    @pl.loop(1, n_dp)
    def _(offset):
        peer = lax.rem(me_d + offset, n_dp)
        pl.semaphore_signal(barrier, inc=1, device_id={"dp": peer}, device_id_type=MESH)

    for neighbour in (left, right):
        pl.semaphore_signal(barrier, inc=1, device_id={"mp": neighbour}, device_id_type=MESH)

    start = jnp.int32(0)
    for i in range(n_dp):
        start = start + jnp.where(i < me_d, counts[i], 0)
    count = counts[me_d]
    wanted = [
        jnp.where(s < count, dest[lax.rem(start + s, n_dp)], -1) for s in range(in_slots)
    ]

    @pl.loop(0, n_dp)
    def _(d):
        slot = jnp.int32(0)
        for s in range(1, in_slots):
            slot = slot + jnp.where(wanted[s] == d, s, 0)
        slots[d] = jnp.minimum(slot, in_slots - 1)

    local[0].wait()
    local[1].wait()

    def pack(g):
        @pl.loop(0, n_dp, unroll=4)
        def _(d):
            send[d, g * rows : (g + 1) * rows, :] = hid[slots[d], g * rows : (g + 1) * rows, :]

        recvs[g][me_d] = send[me_d, g * rows : (g + 1) * rows, :]

    def dispatch(g):
        @pl.loop(1, n_dp)
        def _(offset):
            peer = lax.rem(me_d + offset, n_dp)
            pltpu.make_async_remote_copy(
                send.at[peer, pl.ds(g * rows, rows)], recvs[g].at[me_d], send_sem.at[g], move_sem.at[g],
                device_id={"dp": peer}, device_id_type=MESH,
            ).start()

    pack(0)

    @pl.loop(0, n_dp)
    def _(d):
        seg_send[d] = seg[pl.ds(slots[d], 1), :]

    seg_recv[me_d] = seg_send[me_d]
    pl.semaphore_wait(barrier, n_dp + 1)
    dispatch(0)

    @pl.loop(1, n_dp)
    def _(offset):
        peer = lax.rem(me_d + offset, n_dp)
        pltpu.make_async_remote_copy(
            seg_send.at[peer], seg_recv.at[me_d], seg_sem.at[0], seg_sem.at[1],
            device_id={"dp": peer}, device_id_type=MESH,
        ).start()

    for g in range(1, GROUPS):
        pack(g)
        dispatch(g)

    mine = jnp.int32(0)
    for j in range(n_dp):
        mine = mine + jnp.where(dest[j] == me_d, j, 0)
    finish = jnp.int32(0)
    owners = [jnp.int32(0)] * kept
    for i in range(n_dp):
        finish = finish + counts[i]
        owners = [o + jnp.where(finish <= k * n_dp + mine, 1, 0) for k, o in enumerate(owners)]
    for k in range(kept):
        sources[k] = jnp.minimum(owners[k], n_dp - 1)

    gains[...] = gain[...].astype(f32)
    keys[...] = jnp.zeros_like(keys)
    values[...] = jnp.zeros_like(values)

    def ring_copy(z, g, p, s, way):
        block = ag.at[z, g, pl.ds(p * piece, piece)]
        return pltpu.make_async_remote_copy(
            block, block, ring_send.at[way, g], ring_recv.at[way, g, s - 1, p],
            device_id={"mp": right if way == 0 else left}, device_id_type=MESH,
        )

    def project(z, g, first=False):
        a = lax.rem(g, 2)
        x = ag[z, g].astype(f32)
        normed = (x * gains[pl.ds(z, 1), :]).astype(bf16)
        at = pl.ds(pl.multiple_of(z * width, width), width)
        queries = jnp.dot(normed, wq[at, :], preferred_element_type=f32)
        pieces = jnp.dot(normed, wkv[at, :], preferred_element_type=f32)
        sums = x[:, :HD] * x[:, :HD]
        for c in range(HD, width, HD):
            sums = sums + x[:, c : c + HD] * x[:, c : c + HD]
        if first:
            acc[a, :, : 2 * HD] = queries
            acc[a, :, 2 * HD :] = pieces
            squares[a] = sums
        else:
            acc[a, :, : 2 * HD] += queries
            acc[a, :, 2 * HD :] += pieces
            squares[a] += sums

    def open_group(g):
        pltpu.make_async_copy(
            recvs[g].at[pl.ds(0, n_dp - 1)], recvs[g].at[pl.ds(0, n_dp - 1)], move_sem.at[g]
        ).wait()
        for k in range(kept):
            ag[me_z, g, k * rows : (k + 1) * rows, :] = recvs[g][sources[k]]
        for p in range(2):
            for way in range(2):
                ring_copy(me_z, g, p, 1, way).start()
        if g == 0:
            local[2].wait()
            local[3].wait()

    def ring_step(g, s, late):
        from_left = lax.rem(me_z + n_mp - s, n_mp)
        from_right = lax.rem(me_z + s, n_mp)

        def arrive(p, way):
            z = from_left if way == 0 else from_right
            ring_copy(z, g, p, s, way).wait_recv()

        def forward(p, way):
            z = from_left if way == 0 else from_right
            ring_copy(z, g, p, s + 1, way).start()

        def both(p, way):
            arrive(p, way)
            forward(p, way)

        if not late:
            for p, way in ((0, 0), (1, 1), (1, 0), (0, 1)):
                both(p, way)
        else:
            for p, way in ((0, 0), (1, 1)):
                arrive(p, way)

                @pl.when(s < far)
                def _():
                    forward(p, way)

            @pl.when(s < far)
            def _():
                for p, way in ((1, 0), (0, 1)):
                    arrive(p, way)

                    @pl.when(s < far - 1)
                    def _():
                        forward(p, way)

        project(from_left, g)
        if not late:
            project(from_right, g)
        else:

            @pl.when(s < far)
            def _():
                project(from_right, g)

    def kv_copy(g):
        return pltpu.make_async_remote_copy(
            kv_mine.at[g], kv_theirs.at[g], kv_send.at[g], kv_recv.at[g],
            device_id={"mp": partner}, device_id_type=MESH,
        )

    def rotated(tensor, g):
        return (
            tensor * tables[g, :, :HD] + pltpu.roll(tensor, HALF, 1) * tables[g, :, HD:]
        ).astype(bf16)

    def close_group(g):
        a = lax.rem(g, 2)
        total = jnp.sum(squares[a], axis=1, keepdims=True)
        scale = lax.rsqrt(total / (n_mp * width) + epsilon)
        kv_mine[g] = (scale * acc[a, :, 2 * HD :]).astype(bf16)
        for h in range(2):
            q_rot[h] = rotated(scale * acc[a, :, h * HD : (h + 1) * HD], g)
        kv_copy(g).start()

    def attend(g):
        kv_copy(g).wait_recv()
        own = kv_mine[g].astype(f32)
        other = kv_theirs[g].astype(f32)
        upper = odd == 1
        leading = jnp.where(upper, other, own)
        trailing = jnp.where(upper, own, other)
        low = lax.broadcasted_iota(jnp.int32, own.shape, 1) < HALF
        key_raw = jnp.where(low, leading, pltpu.roll(trailing, HALF, 1))
        value = jnp.where(low, pltpu.roll(leading, HALF, 1), trailing).astype(bf16)
        key = rotated(key_raw, g)
        at = pl.ds(pl.multiple_of(g * rows, rows), rows)
        for k in range(kept):
            part = slice(k * rows, (k + 1) * rows)
            keys[k, at, :] = key[part]
            values[k, at, :] = value[part]
        for k in range(kept):
            part = slice(k * rows, (k + 1) * rows)
            query = jnp.concatenate([q_rot[0, part], q_rot[1, part]], axis=0)
            scores = lax.dot_general(
                query, keys[k], (((1,), (1,)), ((), ())), preferred_element_type=f32
            ) * HD ** (-0.5)
            visible = masks[g, part]
            visible = jnp.concatenate([visible, visible], axis=0)
            scores = jnp.where(visible > 0.5, scores, MASKED)
            weights = jnp.exp(scores - jnp.max(scores, axis=1, keepdims=True))
            shares = (weights / jnp.sum(weights, axis=1, keepdims=True)).astype(bf16)
            mixture = jnp.dot(shares, values[k], preferred_element_type=f32).astype(bf16)
            out[k, at, :HD] = mixture[:rows]
            out[k, at, HD:] = mixture[rows:]

    def prepare():
        pltpu.make_async_copy(
            seg_recv.at[pl.ds(0, n_dp - 1)], seg_recv.at[pl.ds(0, n_dp - 1)], seg_sem.at[1]
        ).wait()
        shape = (block_len, block_len)
        i = lax.broadcasted_iota(jnp.int32, shape, 0)
        j = lax.broadcasted_iota(jnp.int32, shape, 1)
        for k in range(kept):
            across = jnp.broadcast_to(seg_recv[sources[k]].astype(f32), shape)
            same = across == across.T
            position = jnp.sum(jnp.where(same & (j < i), 1.0, 0.0), axis=1, keepdims=True)
            visible = jnp.where(same & (j <= i), 1.0, 0.0)
            chosen = jnp.where(j.astype(f32) == position, 1.0, 0.0)
            turned = jnp.dot(
                chosen, table[...], precision=lax.Precision.HIGHEST, preferred_element_type=f32
            )
            for g in range(GROUPS):
                tables[g, k * rows : (k + 1) * rows, :] = turned[g * rows : (g + 1) * rows]
                masks[g, k * rows : (k + 1) * rows, :] = visible[g * rows : (g + 1) * rows]

    @pl.loop(0, GROUPS + 1)
    def _(turn):
        for g in range(GROUPS):

            @pl.when(turn == g)
            def _():
                open_group(g)

        @pl.when(turn < GROUPS)
        def _():
            project(me_z, turn, first=True)

        @pl.loop(1, near + 1)
        def _(s):
            @pl.when(turn > 0)
            def _():
                ring_step(turn - 1, s + near, True)

            @pl.when(turn < GROUPS)
            def _():
                ring_step(turn, s, False)

            @pl.when((s == 1) & (turn == 0))
            def _():
                prepare()

            @pl.when((s == near) & (turn > 1))
            def _():
                attend(turn - 2)

        @pl.when(turn > 0)
        def _():
            close_group(turn - 1)

    attend(GROUPS - 1)

    for g in range(GROUPS):
        moved = send.at[pl.ds(0, n_dp - 1), pl.ds(0, rows)]
        pltpu.make_async_copy(moved, moved, send_sem.at[g]).wait()
        passed = ag.at[pl.ds(0, n_mp - 1), 0, pl.ds(0, piece)]
        for way in range(2):
            pltpu.make_async_copy(passed, passed, ring_send.at[way, g]).wait()
        kv_copy(g).wait_send()
    pltpu.make_async_copy(
        seg_send.at[pl.ds(0, n_dp - 1)], seg_send.at[pl.ds(0, n_dp - 1)], seg_sem.at[0]
    ).wait()


def on_device(n_dp, n_mp, hidden, segments, counts, dest_order, norm_gain, q_weight, kv_weight):
    in_slots, block_len = segments.shape
    width = hidden.shape[1]
    kept = in_slots // 2
    rows = block_len // GROUPS
    group_rows = kept * rows
    depth = q_weight.shape[0]
    vmem, smem = (pl.BlockSpec(memory_space=space) for space in (pltpu.VMEM, pltpu.SMEM))
    anywhere = pl.BlockSpec(memory_space=pl.ANY)
    dma = pltpu.SemaphoreType.DMA
    result = pl.pallas_call(
        functools.partial(kernel, n_dp, n_mp),
        out_shape=jax.ShapeDtypeStruct((kept, block_len, width), bf16),
        in_specs=[anywhere, anywhere, smem, smem, vmem, anywhere, anywhere, vmem],
        out_specs=vmem,
        scratch_shapes=[
            pltpu.VMEM((in_slots, block_len, width), bf16),
            pltpu.VMEM((in_slots, block_len), jnp.int32),
            pltpu.VMEM((depth, 2 * HD), bf16),
            pltpu.VMEM((depth, HD), bf16),
            pltpu.VMEM((n_dp, block_len, width), bf16),
            pltpu.VMEM((n_dp, 1, block_len), jnp.int32),
            pltpu.VMEM((n_dp, 1, block_len), jnp.int32),
            *[pltpu.VMEM((n_dp, rows, width), bf16)] * GROUPS,
            pltpu.VMEM((n_mp, GROUPS, group_rows, width), bf16),
            pltpu.VMEM((2, group_rows, 3 * HD), f32),
            pltpu.VMEM((2, group_rows, HD), f32),
            pltpu.VMEM((GROUPS, group_rows, HD), bf16),
            pltpu.VMEM((GROUPS, group_rows, HD), bf16),
            pltpu.VMEM((2, group_rows, HD), bf16),
            pltpu.VMEM((kept, block_len, HD), bf16),
            pltpu.VMEM((kept, block_len, HD), bf16),
            pltpu.VMEM((GROUPS, group_rows, 2 * HD), f32),
            pltpu.VMEM((GROUPS, group_rows, HD), f32),
            pltpu.VMEM((n_mp, width), f32),
            pltpu.SMEM((n_dp,), jnp.int32),
            pltpu.SMEM((kept,), jnp.int32),
            dma((4,)),
            dma((GROUPS,)),
            dma((GROUPS,)),
            dma((2,)),
            dma((2, GROUPS)),
            dma((2, GROUPS, n_mp // 2, 2)),
            dma((GROUPS,)),
            dma((GROUPS,)),
        ],
        compiler_params=pltpu.CompilerParams(
            collective_id=0, has_side_effects=True, vmem_limit_bytes=60 * 1024 * 1024
        ),
        name="move_gather_attend",
    )(
        hidden.reshape(in_slots, block_len, width),
        segments,
        counts,
        dest_order,
        norm_gain.reshape(n_mp, width),
        q_weight,
        kv_weight,
        jnp.asarray(rope_table(block_len)),
    )
    return result.reshape(kept * block_len, width)


def solution(mesh):
    in_specs = (P("dp", "mp"), P("dp", None), P(), P(), P(), P(None, "mp"), P(None, "mp"))
    return jax.shard_map(
        functools.partial(on_device, mesh.shape["dp"], mesh.shape["mp"]),
        mesh=mesh,
        in_specs=in_specs,
        out_specs=P("dp", "mp"),
        check_vma=False,
    )
```

time: 245 us -> 146 us (0.60)
  the two profiles are of different devices: /device:TPU:24 before, /device:TPU:2 now
where the time goes in v1:
time: 146 us; the launch traced here: 145 us
  Pallas kernels  142 us (97%)
  local copies, waits for them, and re-layouts  3.17 us (2%)
    pallas_call x1, Pallas kernels, on_device(): pl.pallas_call(functools.partial(kernel, n_dp, n_mp), out_shape=jax.Shape...  142 us

profile of v1, /device:TPU:2, one launch (start us, length us, event | category | flops | bytes accessed | tf_op | source)
XLA Modules:
  0.0 145.4 jit_solution(8521696636445071552)
XLA Ops:
  0.0 1.3 reshape.10.gain
  1.3 142.2 %move_gather_attend.1 = bf16[8,128,256]{2,1,0:T(8,128)(2,1)} custom-call(bf16[16,128,256]{2,1,0:T(8,128)(2,1)} %bitcast.3, s32[16,128]{1,0:T(8,128)} %segments.1, s32[32]{0:T(128)} %counts.1, s32[32]{0:T(128)} %dest.1, bf16[16,256]{1,0:T(8,128)(2,1)} %reshape.10.gain, bf16[4096,256]{1,0:T(8,128)(2,1)} %q_weight.1, bf16[4096,128]{1,0:T(8,128)(2,1)} %kv_weight.1, ...), custom_call_target="tpu_custom_call" | custom-call | tf_op jit(solution)/shard_map/move_gather_attend/pallas_call | solution.py:353
  143.5 1.9 %copy.10 = bf16[1024,256]{1,0:T(8,128)(2,1)} copy(bf16[1024,256]{1,0:T(8,128)(2,1)} %bitcast.2) | data formatting | bytes 1048576

commit v2 on v1

--- a/solution.py
+++ b/solution.py
@@ -11,6 +11,7 @@
 HD = 128
 HALF = HD // 2
 GROUPS = 4
+LAG = 1
 epsilon = 1e-05
 rope_base = 500000.0
 MASKED = -1e30
@@ -26,22 +27,20 @@
     return np.concatenate([cosine, cosine, -sine, sine], axis=1).astype(np.float32)
 
 
-def kernel(
-    n_dp, n_mp, hidden, segments, counts, dest, gain, q_weight, kv_weight, table, out,
-    hid, seg, wq, wkv, send, seg_send, seg_recv, recv0, recv1, recv2, recv3,
-    ag, acc, squares, kv_mine, kv_theirs, q_rot, keys, values, tables, masks, gains, slots, sources,
-    local_sem, send_sem, move_sem, seg_sem, ring_send, ring_recv, kv_send, kv_recv,
-):
-    recvs = (recv0, recv1, recv2, recv3)
+def kernel(n_dp, n_mp, hidden, segments, counts, dest, gain, q_weight, kv_weight, table, out, *scratch):
+    hid, seg, wq, wkv, send, seg_send, seg_recv, *recvs = scratch[: 7 + GROUPS]
+    (
+        ag, acc, squares, kv_mine, kv_theirs, q_rot, keys, values, tables, masks, gains, done, slots, sources,
+        local_sem, send_sem, move_sem, seg_sem, ring_send, ring_recv, kv_send, kv_recv, out_sem,
+    ) = scratch[7 + GROUPS :]
     me_d = lax.axis_index("dp")
     me_z = lax.axis_index("mp")
     in_slots, block_len, width = hid.shape
     kept = in_slots // 2
     rows = block_len // GROUPS
     group_rows = kept * rows
-    piece = group_rows // 2
+    half = group_rows // 2
     far = n_mp // 2
-    near = far // 2
     right = lax.rem(me_z + 1, n_mp)
     left = lax.rem(me_z + n_mp - 1, n_mp)
     odd = lax.rem(me_z, 2)
@@ -137,31 +136,32 @@
     keys[...] = jnp.zeros_like(keys)
     values[...] = jnp.zeros_like(values)
 
-    def ring_copy(z, g, p, s, way):
-        block = ag.at[z, g, pl.ds(p * piece, piece)]
+    def ring_copy(z, g, s, way, whole):
+        block = ag.at[z, g] if whole else ag.at[z, g, pl.ds(way * half, half)]
         return pltpu.make_async_remote_copy(
-            block, block, ring_send.at[way, g], ring_recv.at[way, g, s - 1, p],
+            block, block, ring_send.at[way + (0 if whole else 2)], ring_recv.at[way, g, s - 1],
             device_id={"mp": right if way == 0 else left}, device_id_type=MESH,
         )
 
     def project(z, g, first=False):
-        a = lax.rem(g, 2)
-        x = ag[z, g].astype(f32)
-        normed = (x * gains[pl.ds(z, 1), :]).astype(bf16)
+        raw = ag[z, g]
+        parts, sums = [], None
+        for c in range(width // HD):
+            x = raw[:, c * HD : (c + 1) * HD].astype(f32)
+            parts.append((x * gains[pl.ds(z * (width // HD) + c, 1), :]).astype(bf16))
+            sums = x * x if sums is None else sums + x * x
+        normed = jnp.concatenate(parts, axis=1)
         at = pl.ds(pl.multiple_of(z * width, width), width)
         queries = jnp.dot(normed, wq[at, :], preferred_element_type=f32)
         pieces = jnp.dot(normed, wkv[at, :], preferred_element_type=f32)
-        sums = x[:, :HD] * x[:, :HD]
-        for c in range(HD, width, HD):
-            sums = sums + x[:, c : c + HD] * x[:, c : c + HD]
         if first:
-            acc[a, :, : 2 * HD] = queries
-            acc[a, :, 2 * HD :] = pieces
-            squares[a] = sums
+            acc[g, :, : 2 * HD] = queries
+            acc[g, :, 2 * HD :] = pieces
+            squares[g] = sums
         else:
-            acc[a, :, : 2 * HD] += queries
-            acc[a, :, 2 * HD :] += pieces
-            squares[a] += sums
+            acc[g, :, : 2 * HD] += queries
+            acc[g, :, 2 * HD :] += pieces
+            squares[g] += sums
 
     def open_group(g):
         pltpu.make_async_copy(
@@ -169,57 +169,39 @@
         ).wait()
         for k in range(kept):
             ag[me_z, g, k * rows : (k + 1) * rows, :] = recvs[g][sources[k]]
-        for p in range(2):
-            for way in range(2):
-                ring_copy(me_z, g, p, 1, way).start()
+        for way in range(2):
+            ring_copy(me_z, g, 1, way, True).start()
         if g == 0:
             local[2].wait()
             local[3].wait()
-
-    def ring_step(g, s, late):
+        project(me_z, g, first=True)
+
+    def ring_step(g, s):
         from_left = lax.rem(me_z + n_mp - s, n_mp)
         from_right = lax.rem(me_z + s, n_mp)
-
-        def arrive(p, way):
-            z = from_left if way == 0 else from_right
-            ring_copy(z, g, p, s, way).wait_recv()
-
-        def forward(p, way):
-            z = from_left if way == 0 else from_right
-            ring_copy(z, g, p, s + 1, way).start()
-
-        def both(p, way):
-            arrive(p, way)
-            forward(p, way)
-
-        if not late:
-            for p, way in ((0, 0), (1, 1), (1, 0), (0, 1)):
-                both(p, way)
-        else:
-            for p, way in ((0, 0), (1, 1)):
-                arrive(p, way)
-
-                @pl.when(s < far)
-                def _():
-                    forward(p, way)
+        for way, z in enumerate((from_left, from_right)):
 
             @pl.when(s < far)
             def _():
-                for p, way in ((1, 0), (0, 1)):
-                    arrive(p, way)
-
-                    @pl.when(s < far - 1)
-                    def _():
-                        forward(p, way)
+                ring_copy(z, g, s, way, True).wait_recv()
+
+            @pl.when(s == far)
+            def _():
+                ring_copy(z, g, s, way, False).wait_recv()
+
+            @pl.when(s < far - 1)
+            def _():
+                ring_copy(z, g, s + 1, way, True).start()
+
+            @pl.when(s == far - 1)
+            def _():
+                ring_copy(z, g, s + 1, way, False).start()
 
         project(from_left, g)
-        if not late:
+
+        @pl.when(s < far)
+        def _():
             project(from_right, g)
-        else:
-
-            @pl.when(s < far)
-            def _():
-                project(from_right, g)
 
     def kv_copy(g):
         return pltpu.make_async_remote_copy(
@@ -233,13 +215,16 @@
         ).astype(bf16)
 
     def close_group(g):
-        a = lax.rem(g, 2)
-        total = jnp.sum(squares[a], axis=1, keepdims=True)
+        total = jnp.sum(squares[g], axis=1, keepdims=True)
         scale = lax.rsqrt(total / (n_mp * width) + epsilon)
-        kv_mine[g] = (scale * acc[a, :, 2 * HD :]).astype(bf16)
+        kv_mine[g] = (scale * acc[g, :, 2 * HD :]).astype(bf16)
         for h in range(2):
-            q_rot[h] = rotated(scale * acc[a, :, h * HD : (h + 1) * HD], g)
+            q_rot[g, h] = rotated(scale * acc[g, :, h * HD : (h + 1) * HD], g)
         kv_copy(g).start()
+
+    def out_copy(g):
+        at = pl.ds(pl.multiple_of(g * rows, rows), rows)
+        return pltpu.make_async_copy(done.at[g], out.at[:, at], out_sem.at[g])
 
     def attend(g):
         kv_copy(g).wait_recv()
@@ -259,7 +244,7 @@
             values[k, at, :] = value[part]
         for k in range(kept):
             part = slice(k * rows, (k + 1) * rows)
-            query = jnp.concatenate([q_rot[0, part], q_rot[1, part]], axis=0)
+            query = jnp.concatenate([q_rot[g, 0, part], q_rot[g, 1, part]], axis=0)
             scores = lax.dot_general(
                 query, keys[k], (((1,), (1,)), ((), ())), preferred_element_type=f32
             ) * HD ** (-0.5)
@@ -269,8 +254,9 @@
             weights = jnp.exp(scores - jnp.max(scores, axis=1, keepdims=True))
             shares = (weights / jnp.sum(weights, axis=1, keepdims=True)).astype(bf16)
             mixture = jnp.dot(shares, values[k], preferred_element_type=f32).astype(bf16)
-            out[k, at, :HD] = mixture[:rows]
-            out[k, at, HD:] = mixture[rows:]
+            done[g, k, :, :HD] = mixture[:rows]
+            done[g, k, :, HD:] = mixture[rows:]
+        out_copy(g).start()
 
     def prepare():
         pltpu.make_async_copy(
@@ -292,49 +278,44 @@
                 tables[g, k * rows : (k + 1) * rows, :] = turned[g * rows : (g + 1) * rows]
                 masks[g, k * rows : (k + 1) * rows, :] = visible[g * rows : (g + 1) * rows]
 
-    @pl.loop(0, GROUPS + 1)
+    @pl.loop(0, LAG * (GROUPS - 1) + far + 2)
     def _(turn):
+        @pl.loop(0, GROUPS)
+        def _(g):
+            s = turn - LAG * g
+
+            @pl.when((s >= 1) & (s <= far))
+            def _():
+                ring_step(g, s)
+
+            @pl.when(s == far)
+            def _():
+                close_group(g)
+
+            @pl.when(s == far + 1)
+            def _():
+                attend(g)
+
         for g in range(GROUPS):
 
-            @pl.when(turn == g)
+            @pl.when(turn == LAG * g)
             def _():
                 open_group(g)
 
-        @pl.when(turn < GROUPS)
+        @pl.when(turn == 1)
         def _():
-            project(me_z, turn, first=True)
-
-        @pl.loop(1, near + 1)
-        def _(s):
-            @pl.when(turn > 0)
-            def _():
-                ring_step(turn - 1, s + near, True)
-
-            @pl.when(turn < GROUPS)
-            def _():
-                ring_step(turn, s, False)
-
-            @pl.when((s == 1) & (turn == 0))
-            def _():
-                prepare()
-
-            @pl.when((s == near) & (turn > 1))
-            def _():
-                attend(turn - 2)
-
-        @pl.when(turn > 0)
-        def _():
-            close_group(turn - 1)
-
-    attend(GROUPS - 1)
+            prepare()
 
     for g in range(GROUPS):
         moved = send.at[pl.ds(0, n_dp - 1), pl.ds(0, rows)]
         pltpu.make_async_copy(moved, moved, send_sem.at[g]).wait()
-        passed = ag.at[pl.ds(0, n_mp - 1), 0, pl.ds(0, piece)]
-        for way in range(2):
-            pltpu.make_async_copy(passed, passed, ring_send.at[way, g]).wait()
         kv_copy(g).wait_send()
+        out_copy(g).wait()
+    for way in range(2):
+        passed = ag.at[pl.ds(0, far - 1)]
+        pltpu.make_async_copy(passed, passed, ring_send.at[way]).wait()
+        passed = ag.at[0, pl.ds(0, GROUPS), pl.ds(0, half)]
+        pltpu.make_async_copy(passed, passed, ring_send.at[way + 2]).wait()
     pltpu.make_async_copy(
         seg_send.at[pl.ds(0, n_dp - 1)], seg_send.at[pl.ds(0, n_dp - 1)], seg_sem.at[0]
     ).wait()
@@ -354,7 +335,7 @@
         functools.partial(kernel, n_dp, n_mp),
         out_shape=jax.ShapeDtypeStruct((kept, block_len, width), bf16),
         in_specs=[anywhere, anywhere, smem, smem, vmem, anywhere, anywhere, vmem],
-        out_specs=vmem,
+        out_specs=anywhere,
         scratch_shapes=[
             pltpu.VMEM((in_slots, block_len, width), bf16),
             pltpu.VMEM((in_slots, block_len), jnp.int32),
@@ -365,24 +346,26 @@
             pltpu.VMEM((n_dp, 1, block_len), jnp.int32),
             *[pltpu.VMEM((n_dp, rows, width), bf16)] * GROUPS,
             pltpu.VMEM((n_mp, GROUPS, group_rows, width), bf16),
-            pltpu.VMEM((2, group_rows, 3 * HD), f32),
-            pltpu.VMEM((2, group_rows, HD), f32),
+            pltpu.VMEM((GROUPS, group_rows, 3 * HD), f32),
+            pltpu.VMEM((GROUPS, group_rows, HD), f32),
             pltpu.VMEM((GROUPS, group_rows, HD), bf16),
             pltpu.VMEM((GROUPS, group_rows, HD), bf16),
-            pltpu.VMEM((2, group_rows, HD), bf16),
+            pltpu.VMEM((GROUPS, 2, group_rows, HD), bf16),
             pltpu.VMEM((kept, block_len, HD), bf16),
             pltpu.VMEM((kept, block_len, HD), bf16),
             pltpu.VMEM((GROUPS, group_rows, 2 * HD), f32),
             pltpu.VMEM((GROUPS, group_rows, HD), f32),
-            pltpu.VMEM((n_mp, width), f32),
+            pltpu.VMEM((n_mp * width // HD, HD), f32),
+            pltpu.VMEM((GROUPS, kept, rows, width), bf16),
             pltpu.SMEM((n_dp,), jnp.int32),
             pltpu.SMEM((kept,), jnp.int32),
             dma((4,)),
             dma((GROUPS,)),
             dma((GROUPS,)),
             dma((2,)),
-            dma((2, GROUPS)),
-            dma((2, GROUPS, n_mp // 2, 2)),
+            dma((4,)),
+            dma((2, GROUPS, n_mp // 2)),
+            dma((GROUPS,)),
             dma((GROUPS,)),
             dma((GROUPS,)),
         ],
@@ -395,7 +378,7 @@
         segments,
         counts,
         dest_order,
-        norm_gain.reshape(n_mp, width),
+        norm_gain.reshape(n_mp * width // HD, HD),
         q_weight,
         kv_weight,
         jnp.asarray(rope_table(block_len)),

time: 146 us -> 133 us (0.911)
  Pallas kernels: 142 us -> 131 us
    pallas_call x1, Pallas kernels: 142 us -> 131 us  [on_device(): pl.pallas_call(functools.partial(kernel, n_dp, n_mp), out_shape=jax.Shape...]
where the time goes in v2:
time: 133 us
  Pallas kernels  131 us (98%)
  local copies, waits for them, and re-layouts  1.87 us (1%)
    pallas_call x1, Pallas kernels, on_device(): pl.pallas_call(functools.partial(kernel, n_dp, n_mp), out_shape=jax.Shape...  131 us

profile of v2, /device:TPU:2, one launch (start us, length us, event | category | flops | bytes accessed | tf_op | source)
XLA Modules:
  0.0 133.2 jit_solution(135681563635532717)
XLA Ops:
  0.0 131.3 %move_gather_attend.1 = bf16[8,128,256]{2,1,0:T(8,128)(2,1)} custom-call(bf16[16,128,256]{2,1,0:T(8,128)(2,1)} %bitcast.4, s32[16,128]{1,0:T(8,128)} %segments.1, s32[32]{0:T(128)} %counts.1, s32[32]{0:T(128)} %dest.1, bf16[32,128]{1,0:T(8,128)(2,1)} %bitcast.5, bf16[4096,256]{1,0:T(8,128)(2,1)} %q_weight.1, bf16[4096,128]{1,0:T(8,128)(2,1)} %kv_weight.1, ...), custom_call_target="tpu_custom_call" | custom-call | tf_op jit(solution)/shard_map/move_gather_attend/pallas_call | solution.py:334
  131.3 1.9 %copy.10 = bf16[1024,256]{1,0:T(8,128)(2,1)} copy(bf16[1024,256]{1,0:T(8,128)(2,1)} %bitcast.3) | data formatting | bytes 1048576

commit v3 on v2

--- a/solution.py
+++ b/solution.py
@@ -10,8 +10,9 @@
 
 HD = 128
 HALF = HD // 2
-GROUPS = 4
-LAG = 1
+GROUPS = 8
+PAIR = 2
+READY = 4
 epsilon = 1e-05
 rope_base = 500000.0
 MASKED = -1e30
@@ -30,7 +31,7 @@
 def kernel(n_dp, n_mp, hidden, segments, counts, dest, gain, q_weight, kv_weight, table, out, *scratch):
     hid, seg, wq, wkv, send, seg_send, seg_recv, *recvs = scratch[: 7 + GROUPS]
     (
-        ag, acc, squares, kv_mine, kv_theirs, q_rot, keys, values, tables, masks, gains, done, slots, sources,
+        ag, acc, squares, keys, values, tables, masks, gains, done, slots, sources,
         local_sem, send_sem, move_sem, seg_sem, ring_send, ring_recv, kv_send, kv_recv, out_sem,
     ) = scratch[7 + GROUPS :]
     me_d = lax.axis_index("dp")
@@ -45,12 +46,18 @@
     left = lax.rem(me_z + n_mp - 1, n_mp)
     odd = lax.rem(me_z, 2)
     partner = me_z + 1 - 2 * odd
+    core = lax.rem(me_d, 2)
+    sibling = me_d + 1 - 2 * core
+    across = n_dp // 4
+    side = lax.rem(me_d // across, 2)
+    beside = me_d + across - 2 * across * side
+    quarter = kv_weight.shape[0] // 4
 
     local = [
         pltpu.make_async_copy(hidden, hid, local_sem.at[0]),
         pltpu.make_async_copy(segments, seg, local_sem.at[1]),
         pltpu.make_async_copy(q_weight, wq, local_sem.at[2]),
-        pltpu.make_async_copy(kv_weight, wkv, local_sem.at[3]),
+        pltpu.make_async_copy(kv_weight, wkv.at[:, pl.ds(0, HD)], local_sem.at[3]),
     ]
     for copy in local:
         copy.start()
@@ -107,6 +114,27 @@
 
     seg_recv[me_d] = seg_send[me_d]
     pl.semaphore_wait(barrier, n_dp + 1)
+
+    def kv_part(which):
+        return pl.ds(pl.multiple_of(which * quarter, quarter), quarter)
+
+    def kv_share(which, stage, device):
+        block = wkv.at[kv_part(which), pl.ds(HD, HD)]
+        return pltpu.make_async_remote_copy(
+            block, block, kv_send.at[stage], kv_recv.at[stage],
+            device_id={"dp": device}, device_id_type=MESH,
+        )
+
+    own_part = 2 * side + core
+    kv_fetch = pltpu.make_async_remote_copy(
+        kv_weight.at[kv_part(own_part)], wkv.at[kv_part(own_part), pl.ds(HD, HD)], kv_send.at[0], kv_recv.at[0],
+        device_id={"mp": partner}, device_id_type=MESH,
+    )
+    kv_fetch.start()
+    kv_beside = kv_share(own_part, 1, beside)
+    kv_sibling = kv_share(own_part, 2, sibling)
+    kv_passed = kv_share(2 - 2 * side + core, 3, sibling)
+
     dispatch(0)
 
     @pl.loop(1, n_dp)
@@ -117,7 +145,7 @@
             device_id={"dp": peer}, device_id_type=MESH,
         ).start()
 
-    for g in range(1, GROUPS):
+    for g in range(1, GROUPS // 2):
         pack(g)
         dispatch(g)
 
@@ -163,6 +191,9 @@
             acc[g, :, 2 * HD :] += pieces
             squares[g] += sums
 
+    def around(s):
+        return lax.rem(me_z + n_mp - s, n_mp), lax.rem(me_z + s, n_mp)
+
     def open_group(g):
         pltpu.make_async_copy(
             recvs[g].at[pl.ds(0, n_dp - 1)], recvs[g].at[pl.ds(0, n_dp - 1)], move_sem.at[g]
@@ -171,15 +202,9 @@
             ag[me_z, g, k * rows : (k + 1) * rows, :] = recvs[g][sources[k]]
         for way in range(2):
             ring_copy(me_z, g, 1, way, True).start()
-        if g == 0:
-            local[2].wait()
-            local[3].wait()
-        project(me_z, g, first=True)
 
     def ring_step(g, s):
-        from_left = lax.rem(me_z + n_mp - s, n_mp)
-        from_right = lax.rem(me_z + s, n_mp)
-        for way, z in enumerate((from_left, from_right)):
+        for way, z in enumerate(around(s)):
 
             @pl.when(s < far)
             def _():
@@ -197,39 +222,36 @@
             def _():
                 ring_copy(z, g, s + 1, way, False).start()
 
-        project(from_left, g)
-
-        @pl.when(s < far)
+    def catch_up(g, s):
+        from_left, from_right = around(s)
+
+        @pl.when(s == 0)
+        def _():
+            project(me_z, g, first=True)
+
+        @pl.when(s > 0)
+        def _():
+            project(from_left, g)
+
+        @pl.when((s > 0) & (s < far))
         def _():
             project(from_right, g)
-
-    def kv_copy(g):
-        return pltpu.make_async_remote_copy(
-            kv_mine.at[g], kv_theirs.at[g], kv_send.at[g], kv_recv.at[g],
-            device_id={"mp": partner}, device_id_type=MESH,
-        )
 
     def rotated(tensor, g):
         return (
             tensor * tables[g, :, :HD] + pltpu.roll(tensor, HALF, 1) * tables[g, :, HD:]
         ).astype(bf16)
 
-    def close_group(g):
-        total = jnp.sum(squares[g], axis=1, keepdims=True)
-        scale = lax.rsqrt(total / (n_mp * width) + epsilon)
-        kv_mine[g] = (scale * acc[g, :, 2 * HD :]).astype(bf16)
-        for h in range(2):
-            q_rot[g, h] = rotated(scale * acc[g, :, h * HD : (h + 1) * HD], g)
-        kv_copy(g).start()
-
     def out_copy(g):
         at = pl.ds(pl.multiple_of(g * rows, rows), rows)
         return pltpu.make_async_copy(done.at[g], out.at[:, at], out_sem.at[g])
 
     def attend(g):
-        kv_copy(g).wait_recv()
-        own = kv_mine[g].astype(f32)
-        other = kv_theirs[g].astype(f32)
+        total = jnp.sum(squares[g], axis=1, keepdims=True)
+        scale = lax.rsqrt(total / (n_mp * width) + epsilon)
+        query_rows = [rotated(scale * acc[g, :, h * HD : (h + 1) * HD], g) for h in range(2)]
+        own = (scale * acc[g, :, 2 * HD : 3 * HD]).astype(bf16).astype(f32)
+        other = (scale * acc[g, :, 3 * HD :]).astype(bf16).astype(f32)
         upper = odd == 1
         leading = jnp.where(upper, other, own)
         trailing = jnp.where(upper, own, other)
@@ -242,20 +264,25 @@
             part = slice(k * rows, (k + 1) * rows)
             keys[k, at, :] = key[part]
             values[k, at, :] = value[part]
-        for k in range(kept):
-            part = slice(k * rows, (k + 1) * rows)
-            query = jnp.concatenate([q_rot[g, 0, part], q_rot[g, 1, part]], axis=0)
-            scores = lax.dot_general(
-                query, keys[k], (((1,), (1,)), ((), ())), preferred_element_type=f32
-            ) * HD ** (-0.5)
-            visible = masks[g, part]
-            visible = jnp.concatenate([visible, visible], axis=0)
-            scores = jnp.where(visible > 0.5, scores, MASKED)
-            weights = jnp.exp(scores - jnp.max(scores, axis=1, keepdims=True))
-            shares = (weights / jnp.sum(weights, axis=1, keepdims=True)).astype(bf16)
-            mixture = jnp.dot(shares, values[k], preferred_element_type=f32).astype(bf16)
-            done[g, k, :, :HD] = mixture[:rows]
-            done[g, k, :, HD:] = mixture[rows:]
+        parts = [slice(k * rows, (k + 1) * rows) for k in range(kept)]
+        scores = [
+            lax.dot_general(
+                jnp.concatenate([query_rows[0][part], query_rows[1][part]], axis=0), keys[k],
+                (((1,), (1,)), ((), ())), preferred_element_type=f32,
+            )
+            for k, part in enumerate(parts)
+        ]
+        visible = jnp.concatenate([masks[g, part] for part in parts for _ in range(2)], axis=0)
+        scores = jnp.where(visible > 0.5, jnp.concatenate(scores, axis=0) * HD ** (-0.5), MASKED)
+        weights = jnp.exp(scores - jnp.max(scores, axis=1, keepdims=True))
+        shares = (weights * (1.0 / jnp.sum(weights, axis=1, keepdims=True))).astype(bf16)
+        mixtures = [
+            jnp.dot(shares[2 * k * rows : 2 * (k + 1) * rows], values[k], preferred_element_type=f32)
+            for k in range(kept)
+        ]
+        for k, mixture in enumerate(mixtures):
+            done[g, k, :, :HD] = mixture[:rows].astype(bf16)
+            done[g, k, :, HD:] = mixture[rows:].astype(bf16)
         out_copy(g).start()
 
     def prepare():
@@ -278,39 +305,67 @@
                 tables[g, k * rows : (k + 1) * rows, :] = turned[g * rows : (g + 1) * rows]
                 masks[g, k * rows : (k + 1) * rows, :] = visible[g * rows : (g + 1) * rows]
 
-    @pl.loop(0, LAG * (GROUPS - 1) + far + 2)
+    @pl.loop(0, (GROUPS - 1) // PAIR + far + 1)
     def _(turn):
+        @pl.when(turn == READY)
+        def _():
+            local[2].wait()
+            local[3].wait()
+            kv_sibling.wait_recv()
+            kv_passed.wait_recv()
+
         @pl.loop(0, GROUPS)
         def _(g):
-            s = turn - LAG * g
+            s = turn - g // PAIR
 
             @pl.when((s >= 1) & (s <= far))
             def _():
                 ring_step(g, s)
 
+            older = turn - READY
+
+            @pl.when((older >= 0) & (older < READY - g // PAIR))
+            def _():
+                catch_up(g, older)
+
+            @pl.when((turn >= READY) & (s >= 0) & (s <= far))
+            def _():
+                catch_up(g, s)
+
             @pl.when(s == far)
             def _():
-                close_group(g)
-
-            @pl.when(s == far + 1)
-            def _():
                 attend(g)
 
         for g in range(GROUPS):
 
-            @pl.when(turn == LAG * g)
+            @pl.when(turn == g // PAIR)
             def _():
                 open_group(g)
 
+        @pl.when(turn == 0)
+        def _():
+            kv_fetch.wait_recv()
+            kv_beside.start()
+            kv_sibling.start()
+            for g in range(GROUPS // 2, GROUPS):
+                pack(g)
+                dispatch(g)
+
         @pl.when(turn == 1)
         def _():
             prepare()
+
+        @pl.when(turn == READY - 2)
+        def _():
+            kv_beside.wait_recv()
+            kv_passed.start()
 
     for g in range(GROUPS):
         moved = send.at[pl.ds(0, n_dp - 1), pl.ds(0, rows)]
         pltpu.make_async_copy(moved, moved, send_sem.at[g]).wait()
-        kv_copy(g).wait_send()
         out_copy(g).wait()
+    for copy in (kv_fetch, kv_beside, kv_sibling, kv_passed):
+        copy.wait_send()
     for way in range(2):
         passed = ag.at[pl.ds(0, far - 1)]
         pltpu.make_async_copy(passed, passed, ring_send.at[way]).wait()
@@ -340,17 +395,14 @@
             pltpu.VMEM((in_slots, block_len, width), bf16),
             pltpu.VMEM((in_slots, block_len), jnp.int32),
             pltpu.VMEM((depth, 2 * HD), bf16),
-            pltpu.VMEM((depth, HD), bf16),
+            pltpu.VMEM((depth, 2 * HD), bf16),
             pltpu.VMEM((n_dp, block_len, width), bf16),
             pltpu.VMEM((n_dp, 1, block_len), jnp.int32),
             pltpu.VMEM((n_dp, 1, block_len), jnp.int32),
             *[pltpu.VMEM((n_dp, rows, width), bf16)] * GROUPS,
             pltpu.VMEM((n_mp, GROUPS, group_rows, width), bf16),
-            pltpu.VMEM((GROUPS, group_rows, 3 * HD), f32),
+            pltpu.VMEM((GROUPS, group_rows, 4 * HD), f32),
             pltpu.VMEM((GROUPS, group_rows, HD), f32),
-            pltpu.VMEM((GROUPS, group_rows, HD), bf16),
-            pltpu.VMEM((GROUPS, group_rows, HD), bf16),
-            pltpu.VMEM((GROUPS, 2, group_rows, HD), bf16),
             pltpu.VMEM((kept, block_len, HD), bf16),
             pltpu.VMEM((kept, block_len, HD), bf16),
             pltpu.VMEM((GROUPS, group_rows, 2 * HD), f32),
@@ -365,8 +417,8 @@
             dma((2,)),
             dma((4,)),
             dma((2, GROUPS, n_mp // 2)),
-            dma((GROUPS,)),
-            dma((GROUPS,)),
+            dma((4,)),
+            dma((4,)),
             dma((GROUPS,)),
         ],
         compiler_params=pltpu.CompilerParams(

time: 133 us -> 119 us (0.89)
  the two profiles are of different devices: /device:TPU:2 before, /device:TPU:24 now
where the time goes in v3:
time: 119 us
  Pallas kernels  117 us (98%)
  local copies, waits for them, and re-layouts  1.87 us (2%)
    pallas_call x1, Pallas kernels, on_device(): pl.pallas_call(functools.partial(kernel, n_dp, n_mp), out_shape=jax.Shape...  117 us

profile of v3, /device:TPU:24, one launch (start us, length us, event | category | flops | bytes accessed | tf_op | source)
XLA Modules:
  0.0 118.6 jit_solution(3411953285286494161)
XLA Ops:
  0.0 116.8 %move_gather_attend.1 = bf16[8,128,256]{2,1,0:T(8,128)(2,1)} custom-call(bf16[16,128,256]{2,1,0:T(8,128)(2,1)} %bitcast.4, s32[16,128]{1,0:T(8,128)} %segments.1, s32[32]{0:T(128)} %counts.1, s32[32]{0:T(128)} %dest.1, bf16[32,128]{1,0:T(8,128)(2,1)} %bitcast.5, bf16[4096,256]{1,0:T(8,128)(2,1)} %q_weight.1, bf16[4096,128]{1,0:T(8,128)(2,1)} %kv_weight.1, ...), custom_call_target="tpu_custom_call" | custom-call | tf_op jit(solution)/shard_map/move_gather_attend/pallas_call | solution.py:389
  116.8 1.9 %copy.10 = bf16[1024,256]{1,0:T(8,128)(2,1)} copy(bf16[1024,256]{1,0:T(8,128)(2,1)} %bitcast.3) | data formatting | bytes 1048576

commit v4 on v3

--- a/solution.py
+++ b/solution.py
@@ -11,7 +11,7 @@
 HD = 128
 HALF = HD // 2
 GROUPS = 8
-PAIR = 2
+EARLY = 4
 READY = 4
 epsilon = 1e-05
 rope_base = 500000.0
@@ -28,11 +28,15 @@
     return np.concatenate([cosine, cosine, -sine, sine], axis=1).astype(np.float32)
 
 
+def opens(g):
+    return g // 2
+
+
 def kernel(n_dp, n_mp, hidden, segments, counts, dest, gain, q_weight, kv_weight, table, out, *scratch):
     hid, seg, wq, wkv, send, seg_send, seg_recv, *recvs = scratch[: 7 + GROUPS]
     (
-        ag, acc, squares, keys, values, tables, masks, gains, done, slots, sources,
-        local_sem, send_sem, move_sem, seg_sem, ring_send, ring_recv, kv_send, kv_recv, out_sem,
+        ag, acc, squares, keys, values, tables, masks, gains, slots, sources,
+        local_sem, send_sem, move_sem, seg_sem, ring_send, ring_recv, kv_send, kv_recv,
     ) = scratch[7 + GROUPS :]
     me_d = lax.axis_index("dp")
     me_z = lax.axis_index("mp")
@@ -145,7 +149,7 @@
             device_id={"dp": peer}, device_id_type=MESH,
         ).start()
 
-    for g in range(1, GROUPS // 2):
+    for g in range(1, EARLY):
         pack(g)
         dispatch(g)
 
@@ -202,6 +206,8 @@
             ag[me_z, g, k * rows : (k + 1) * rows, :] = recvs[g][sources[k]]
         for way in range(2):
             ring_copy(me_z, g, 1, way, True).start()
+        if opens(g) >= READY:
+            project(me_z, g, first=True)
 
     def ring_step(g, s):
         for way, z in enumerate(around(s)):
@@ -241,10 +247,6 @@
         return (
             tensor * tables[g, :, :HD] + pltpu.roll(tensor, HALF, 1) * tables[g, :, HD:]
         ).astype(bf16)
-
-    def out_copy(g):
-        at = pl.ds(pl.multiple_of(g * rows, rows), rows)
-        return pltpu.make_async_copy(done.at[g], out.at[:, at], out_sem.at[g])
 
     def attend(g):
         total = jnp.sum(squares[g], axis=1, keepdims=True)
@@ -281,9 +283,8 @@
             for k in range(kept)
         ]
         for k, mixture in enumerate(mixtures):
-            done[g, k, :, :HD] = mixture[:rows].astype(bf16)
-            done[g, k, :, HD:] = mixture[rows:].astype(bf16)
-        out_copy(g).start()
+            out[k, at, :HD] = mixture[:rows].astype(bf16)
+            out[k, at, HD:] = mixture[rows:].astype(bf16)
 
     def prepare():
         pltpu.make_async_copy(
@@ -305,7 +306,7 @@
                 tables[g, k * rows : (k + 1) * rows, :] = turned[g * rows : (g + 1) * rows]
                 masks[g, k * rows : (k + 1) * rows, :] = visible[g * rows : (g + 1) * rows]
 
-    @pl.loop(0, (GROUPS - 1) // PAIR + far + 1)
+    @pl.loop(0, opens(GROUPS - 1) + far + 1)
     def _(turn):
         @pl.when(turn == READY)
         def _():
@@ -316,7 +317,7 @@
 
         @pl.loop(0, GROUPS)
         def _(g):
-            s = turn - g // PAIR
+            s = turn - opens(g)
 
             @pl.when((s >= 1) & (s <= far))
             def _():
@@ -324,11 +325,11 @@
 
             older = turn - READY
 
-            @pl.when((older >= 0) & (older < READY - g // PAIR))
+            @pl.when((older >= 0) & (older < READY - opens(g)))
             def _():
                 catch_up(g, older)
 
-            @pl.when((turn >= READY) & (s >= 0) & (s <= far))
+            @pl.when((turn >= READY) & (s >= 1) & (s <= far))
             def _():
                 catch_up(g, s)
 
@@ -338,7 +339,7 @@
 
         for g in range(GROUPS):
 
-            @pl.when(turn == g // PAIR)
+            @pl.when(turn == opens(g))
             def _():
                 open_group(g)
 
@@ -347,7 +348,7 @@
             kv_fetch.wait_recv()
             kv_beside.start()
             kv_sibling.start()
-            for g in range(GROUPS // 2, GROUPS):
+            for g in range(EARLY, GROUPS):
                 pack(g)
                 dispatch(g)
 
@@ -363,7 +364,6 @@
     for g in range(GROUPS):
         moved = send.at[pl.ds(0, n_dp - 1), pl.ds(0, rows)]
         pltpu.make_async_copy(moved, moved, send_sem.at[g]).wait()
-        out_copy(g).wait()
     for copy in (kv_fetch, kv_beside, kv_sibling, kv_passed):
         copy.wait_send()
     for way in range(2):
@@ -388,9 +388,9 @@
     dma = pltpu.SemaphoreType.DMA
     result = pl.pallas_call(
         functools.partial(kernel, n_dp, n_mp),
-        out_shape=jax.ShapeDtypeStruct((kept, block_len, width), bf16),
+        out_shape=pltpu.VMEM((kept, block_len, width), bf16),
         in_specs=[anywhere, anywhere, smem, smem, vmem, anywhere, anywhere, vmem],
-        out_specs=anywhere,
+        out_specs=vmem,
         scratch_shapes=[
             pltpu.VMEM((in_slots, block_len, width), bf16),
             pltpu.VMEM((in_slots, block_len), jnp.int32),
@@ -408,7 +408,6 @@
             pltpu.VMEM((GROUPS, group_rows, 2 * HD), f32),
             pltpu.VMEM((GROUPS, group_rows, HD), f32),
             pltpu.VMEM((n_mp * width // HD, HD), f32),
-            pltpu.VMEM((GROUPS, kept, rows, width), bf16),
             pltpu.SMEM((n_dp,), jnp.int32),
             pltpu.SMEM((kept,), jnp.int32),
             dma((4,)),
@@ -419,7 +418,6 @@
             dma((2, GROUPS, n_mp // 2)),
             dma((4,)),
             dma((4,)),
-            dma((GROUPS,)),
         ],
         compiler_params=pltpu.CompilerParams(
             collective_id=0, has_side_effects=True, vmem_limit_bytes=60 * 1024 * 1024

time: 119 us -> 117 us (0.983)
  no operation moved by 1% of the time
where the time goes in v4:
time: 117 us
  Pallas kernels  116 us (99%)
    pallas_call x1, Pallas kernels, on_device(): pl.pallas_call(functools.partial(kernel, n_dp, n_mp), out_shape=pltpu.VME...  116 us

profile of v4, /device:TPU:24, one launch (start us, length us, event | category | flops | bytes accessed | tf_op | source)
XLA Modules:
  0.0 116.9 jit_solution(16657415648608437491)
XLA Ops:
  0.0 116.1 %move_gather_attend.1 = bf16[8,128,256]{2,1,0:T(8,128)(2,1)S(1)} custom-call(bf16[16,128,256]{2,1,0:T(8,128)(2,1)} %bitcast.4, s32[16,128]{1,0:T(8,128)} %segments.1, s32[32]{0:T(128)} %counts.1, s32[32]{0:T(128)} %dest.1, bf16[32,128]{1,0:T(8,128)(2,1)} %bitcast.5, bf16[4096,256]{1,0:T(8,128)(2,1)} %q_weight.1, bf16[4096,128]{1,0:T(8,128)(2,1)} %kv_weight.1, ...), custom_call_target="tpu_custom_call" | custom-call | tf_op jit(solution)/shard_map/move_gather_attend/pallas_call | solution.py:389
  116.1 0.8 copy.10

commit v5 on v4

--- a/solution.py
+++ b/solution.py
@@ -32,10 +32,10 @@
     return g // 2
 
 
-def kernel(n_dp, n_mp, hidden, segments, counts, dest, gain, q_weight, kv_weight, table, out, *scratch):
+def kernel(n_dp, n_mp, hidden, segments, counts, dest, gain_in, q_weight, kv_weight, table_in, out, *scratch):
     hid, seg, wq, wkv, send, seg_send, seg_recv, *recvs = scratch[: 7 + GROUPS]
     (
-        ag, acc, squares, keys, values, tables, masks, gains, slots, sources,
+        ag, acc, squares, keys, values, tables, masks, gains, gain, table, slots, sources,
         local_sem, send_sem, move_sem, seg_sem, ring_send, ring_recv, kv_send, kv_recv,
     ) = scratch[7 + GROUPS :]
     me_d = lax.axis_index("dp")
@@ -62,19 +62,20 @@
         pltpu.make_async_copy(segments, seg, local_sem.at[1]),
         pltpu.make_async_copy(q_weight, wq, local_sem.at[2]),
         pltpu.make_async_copy(kv_weight, wkv.at[:, pl.ds(0, HD)], local_sem.at[3]),
+        pltpu.make_async_copy(gain_in, gain, local_sem.at[4]),
+        pltpu.make_async_copy(table_in, table, local_sem.at[5]),
     ]
     for copy in local:
         copy.start()
 
     barrier = pltpu.get_barrier_semaphore()
+    for neighbour in (left, right):
+        pl.semaphore_signal(barrier, inc=1, device_id={"mp": neighbour}, device_id_type=MESH)
 
     @pl.loop(1, n_dp)
     def _(offset):
         peer = lax.rem(me_d + offset, n_dp)
         pl.semaphore_signal(barrier, inc=1, device_id={"dp": peer}, device_id_type=MESH)
-
-    for neighbour in (left, right):
-        pl.semaphore_signal(barrier, inc=1, device_id={"mp": neighbour}, device_id_type=MESH)
 
     start = jnp.int32(0)
     for i in range(n_dp):
@@ -164,6 +165,7 @@
     for k in range(kept):
         sources[k] = jnp.minimum(owners[k], n_dp - 1)
 
+    local[4].wait()
     gains[...] = gain[...].astype(f32)
     keys[...] = jnp.zeros_like(keys)
     values[...] = jnp.zeros_like(values)
@@ -287,6 +289,7 @@
             out[k, at, HD:] = mixture[rows:].astype(bf16)
 
     def prepare():
+        local[5].wait()
         pltpu.make_async_copy(
             seg_recv.at[pl.ds(0, n_dp - 1)], seg_recv.at[pl.ds(0, n_dp - 1)], seg_sem.at[1]
         ).wait()
@@ -389,7 +392,7 @@
     result = pl.pallas_call(
         functools.partial(kernel, n_dp, n_mp),
         out_shape=pltpu.VMEM((kept, block_len, width), bf16),
-        in_specs=[anywhere, anywhere, smem, smem, vmem, anywhere, anywhere, vmem],
+        in_specs=[anywhere, anywhere, smem, smem, anywhere, anywhere, anywhere, anywhere],
         out_specs=vmem,
         scratch_shapes=[
             pltpu.VMEM((in_slots, block_len, width), bf16),
@@ -408,9 +411,11 @@
             pltpu.VMEM((GROUPS, group_rows, 2 * HD), f32),
             pltpu.VMEM((GROUPS, group_rows, HD), f32),
             pltpu.VMEM((n_mp * width // HD, HD), f32),
+            pltpu.VMEM((n_mp * width // HD, HD), bf16),
+            pltpu.VMEM((block_len, 2 * HD), f32),
             pltpu.SMEM((n_dp,), jnp.int32),
             pltpu.SMEM((kept,), jnp.int32),
-            dma((4,)),
+            dma((6,)),
             dma((GROUPS,)),
             dma((GROUPS,)),
             dma((2,)),

time: 117 us -> 117 us (level)
  no operation moved by 1% of the time
where the time goes in v5:
time: 117 us
  Pallas kernels  116 us (99%)
    pallas_call x1, Pallas kernels, on_device(): pl.pallas_call(functools.partial(kernel, n_dp, n_mp), out_shape=pltpu.VME...  116 us

profile of v5, /device:TPU:24, one launch (start us, length us, event | category | flops | bytes accessed | tf_op | source)
XLA Modules:
  0.0 116.7 jit_solution(4364668847163698082)
XLA Ops:
  0.0 115.8 %move_gather_attend.1 = bf16[8,128,256]{2,1,0:T(8,128)(2,1)S(1)} custom-call(bf16[16,128,256]{2,1,0:T(8,128)(2,1)} %bitcast.4, s32[16,128]{1,0:T(8,128)} %segments.1, s32[32]{0:T(128)} %counts.1, s32[32]{0:T(128)} %dest.1, bf16[32,128]{1,0:T(8,128)(2,1)} %bitcast.5, bf16[4096,256]{1,0:T(8,128)(2,1)} %q_weight.1, bf16[4096,128]{1,0:T(8,128)(2,1)} %kv_weight.1, ...), custom_call_target="tpu_custom_call" | custom-call | tf_op jit(solution)/shard_map/move_gather_attend/pallas_call | solution.py:392
  115.9 0.8 copy.10
